TPU v7x, 32 devices: a whole 2x2x4 slice. The times are simulated.
32 devices in a mesh: batch: 4 (over x, core), hidden: 2 (over y), width: 4 (over z).
Axes of the slice: x: 2, y: 2, z: 4, core: 2. Of those that a mesh axis runs over, the one named last changes fastest.
Arguments:
- frames: bfloat16 [4, 512, 1280], P('batch', None, 'hidden'), may hold values from -6 to 6
- adapter_weight: bfloat16 [4, 1280, 16384], P(None, 'hidden', 'width'), may hold values from -0.078125 to 0.078125
- text_embed: bfloat16 [512, 16384], P('batch', 'width'), may hold values from -6 to 6
- audio_len: int32 [4], P('batch'), may hold values from 16 to 64, as said below
- text_len: int32 [4], P('batch'), may hold values from 32 to 112, as said below
- norm_gain: bfloat16 [16384], P('width'), may hold values from 0.5 to 1.5
- gate_up: bfloat16 [16384, 2, 26624], P('width', None, ('batch', 'hidden')), may hold values from -0.046875 to 0.046875
- cotangent: bfloat16 [512, 26624], P('width', ('batch', 'hidden')), may hold values from -0.59765625 to 0.59765625
Outputs:
- hidden: bfloat16 [512, 26624], P('width', ('batch', 'hidden'))
- weight_grad: float32 [4, 1280, 16384], P(None, 'hidden', 'width')
Inputs may be any that keep to these rules, and one draw needn't show every extreme that they name: `audio_len`: some sequence holds exactly 16 audio positions and another exactly 64. audio_len + text_len never exceeds 128, and equals it in some sequence.
All inputs are finite; a program needn't handle non-finite values.
Results may differ from a plain program's by a relative error of at most 0.0059.
Values may be sent and summed in bfloat16 or wider, within the bound.
No kernel may reach another device: no remote copies, remote signals or barrier semaphores. Data moves between devices by JAX's collectives and lax.ppermute only.
A program may use at most 256 MiB of HBM per device.

v0:
```python
import jax
import jax.numpy as jnp
from jax import lax
from jax.sharding import PartitionSpec as P

D = 16384
norm_eps = 1e-05


def row_lookup(table, row_index):
    slots = jnp.arange(table.shape[0], dtype=jnp.int32)
    return jnp.sum(jnp.where(row_index[:, None] == slots[None, :], table[None, :], 0), axis=1)


def on_device(
    frames, adapter_weight, text_embed, audio_len, text_len, norm_gain, gate_up, cotangent
):
    rows_here, frame_count, feat_here = frames.shape
    seq_len = frame_count // 4
    width_here = adapter_weight.shape[2]
    tok_here = rows_here * seq_len
    stacked = frames.reshape(tok_here, 4 * feat_here)
    kernel = adapter_weight.reshape(4 * feat_here, width_here)
    partial_audio = jnp.dot(stacked, kernel, preferred_element_type=jnp.float32)
    audio_part = lax.psum(partial_audio, "hidden")
    local_index = jnp.arange(tok_here, dtype=jnp.int32)
    row_index = local_index // seq_len
    positions = local_index % seq_len
    audio_count = row_lookup(audio_len, row_index)
    text_count = row_lookup(text_len, row_index)
    is_audio = positions < audio_count
    is_text = jnp.logical_and(jnp.logical_not(is_audio), positions < audio_count + text_count)
    stream = jnp.where(
        is_audio[:, None],
        audio_part,
        jnp.where(is_text[:, None], text_embed.astype(jnp.float32), jnp.zeros_like(audio_part)),
    )
    sum_squares = lax.psum(jnp.sum(stream * stream, axis=1), "width")
    inv_rms = lax.rsqrt(sum_squares / D + norm_eps)
    unit_stream = stream * inv_rms[:, None]
    gain_vals = norm_gain.astype(jnp.float32)
    normed = (unit_stream * gain_vals[None, :]).astype(jnp.bfloat16)
    weights = gate_up.reshape(width_here, -1)
    half_cols = weights.shape[1] // 2
    partial_pair = jnp.dot(
        lax.all_gather(normed, "batch", axis=0, tiled=True),
        weights,
        preferred_element_type=jnp.float32,
    )
    summed = lax.psum_scatter(partial_pair, "width", scatter_dimension=0, tiled=True)
    gate_vals = summed[:, :half_cols]
    up_vals = summed[:, half_cols:]
    sigmoid_gate = jax.nn.sigmoid(gate_vals)
    silu_gate = gate_vals * sigmoid_gate
    hidden = (silu_gate * up_vals).astype(jnp.bfloat16)
    cot_vals = cotangent.astype(jnp.float32)
    silu_slope = sigmoid_gate * (1.0 + gate_vals * (1.0 - sigmoid_gate))
    grad_pair = jnp.concatenate(
        [
            (cot_vals * up_vals * silu_slope).astype(jnp.bfloat16),
            (cot_vals * silu_gate).astype(jnp.bfloat16),
        ],
        axis=1,
    )
    all_pairs = lax.all_gather(grad_pair, "width", axis=0, tiled=True)
    share_rows = tok_here // lax.axis_size("hidden")
    row_block = all_pairs
    normed_grad = lax.psum_scatter(
        lax.dot_general(
            row_block, weights, (((1,), (1,)), ((), ())), preferred_element_type=jnp.float32
        ),
        ("batch", "hidden"),
        scatter_dimension=0,
        tiled=True,
    )
    share_start = lax.axis_index("hidden") * share_rows
    unit_share = lax.dynamic_slice_in_dim(unit_stream, share_start, share_rows, 0)
    inv_share = lax.dynamic_slice_in_dim(inv_rms, share_start, share_rows, 0)
    audio_share = lax.dynamic_slice_in_dim(is_audio, share_start, share_rows, 0)
    scaled_grad = normed_grad * gain_vals[None, :]
    proj_stat = lax.psum(jnp.sum(unit_share * scaled_grad, axis=1), "width") / D
    stream_grad = (scaled_grad - unit_share * proj_stat[:, None]) * inv_share[:, None]
    audio_grad = jnp.where(audio_share[:, None], stream_grad, jnp.zeros_like(stream_grad)).astype(
        jnp.bfloat16
    )
    all_frames = lax.all_gather(frames, "batch", axis=0, tiled=True)
    all_stacked = all_frames.reshape(-1, 4 * feat_here)
    row_block = all_stacked
    weight_grad = lax.dot_general(
        row_block,
        lax.all_gather(audio_grad, ("batch", "hidden"), axis=0, tiled=True),
        (((0,), (0,)), ((), ())),
        preferred_element_type=jnp.float32,
    )
    return (hidden, weight_grad.reshape(4, feat_here, width_here))


def solution(mesh):
    return jax.shard_map(
        on_device,
        mesh=mesh,
        in_specs=(
            P("batch", None, "hidden"),
            P(None, "hidden", "width"),
            P("batch", "width"),
            P("batch"),
            P("batch"),
            P("width"),
            P("width", None, ("batch", "hidden")),
            P("width", ("batch", "hidden")),
        ),
        out_specs=(P("width", ("batch", "hidden")), P(None, "hidden", "width")),
        check_vma=False,
    )
```

profile of v0, /device:TPU:0, one launch (start us, length us, event | category | flops | bytes accessed | tf_op | source)
XLA Modules:
  0.0 737.0 jit_solution(10051445883625385876)
XLA Ops:
  7.2 0.0 all-reduce.2.cloned.1.call-start
  7.2 1.5 reshape.67
  8.7 11.2 %fusion.8 = f32[128,4096]{1,0:T(8,128)} fusion(bf16[128,2560]{1,0:T(8,128)(2,1)S(1)} %reshape.67, bf16[2560,4096]{1,0:T(8,128)(2,1)} %bitcast.21), kind=kOutput, calls=%fused_computation.27 | convolution fusion | flops 2684354560 | bytes 23724032 | tf_op jit(solution)/shard_map/dot_general | solution.py:24
  19.9 0.0 copy-start.3
  19.9 0.0 copy-start.1
  19.9 0.0 all-reduce.2.cloned.1.call-update
  19.9 0.0 all-gather.5.cloned.1.call-start
  21.3 0.0 copy-done.3
  21.4 64.4 %all-reduce.2.cloned.1.call-done = f32[128,4096]{1,0:T(8,128)} async-done(((f32[128,4096]{1,0:T(8,128)}), f32[128,4096]{1,0:T(8,128)}) %all-reduce.2.cloned.1.call-update) | async-done | bytes 2097168 | tf_op jit(solution)/shard_map/psum | solution.py:25
  85.8 0.0 copy-done.1
  85.8 2.1 multiply_reduce_fusion
  87.9 11.7 %psum.22 = f32[128]{0:T(128)S(1)} all-reduce(f32[128]{0:T(128)S(1)} %multiply_reduce_fusion), channel_id=1, replica_groups=mesh['batch'=4,'hidden'=2,'width'=4] {'width'}, use_global_device_ids=true, to_apply=%region_2.3 | all-reduce | flops 128 | bytes 1024 | tf_op jit(solution)/shard_map/psum | solution.py:38
  99.6 3.2 multiply_convert_fusion
  102.7 0.0 all-gather.5.cloned.1.call-update
  102.8 0.0 reduce-scatter.3.cloned.1.call-start
  102.8 37.4 %copy.10 = bf16[512,8,2,3328]{3,1,2,0:T(8,128)(2,1)} copy(bf16[512,8,2,3328]{3,2,1,0:T(2,128)(2,1)} %bitcast.18) | data formatting | bytes 109051904
  140.2 0.0 all-gather.5.cloned.1.call-done
  140.2 38.9 %fusion.9 = f32[512,6656]{1,0:T(8,128)} fusion(bf16[512,4096]{1,0:T(8,128)(2,1)} %all-gather.5.cloned.1.call-done, bf16[4096,6656]{1,0:T(8,128)(2,1)} %bitcast.19), kind=kOutput, calls=%fused_computation.28 | convolution fusion | flops 27917287424 | bytes 72351744 | tf_op jit(solution)/shard_map/dot_general | solution.py:45
  179.1 0.0 copy-start.2
  179.1 0.0 reduce-scatter.3.cloned.1.call-update
  179.1 0.2 all-gather.7.cloned.1.call-start
  179.4 226.3 %reduce-scatter.3.cloned.1.call-done = f32[128,6656]{1,0:T(8,128)} async-done(((f32[512,6656]{1,0:T(8,128)}), f32[128,6656]{1,0:T(8,128)}) %reduce-scatter.3.cloned.1.call-update) | async-done | bytes 3407888 | tf_op jit(solution)/shard_map/reduce_scatter | solution.py:50
  405.7 0.0 copy-done.2
  405.7 3.9 fusion.1
  409.5 1.3 pad_maximum_fusion
  410.8 0.0 all-gather.7.cloned.1.call-update
  410.9 0.0 reduce-scatter.5.cloned.1.call-start
  410.9 125.0 %all-gather.7.cloned.1.call-done = bf16[512,6656]{1,0:T(8,128)(2,1)} async-done(((bf16[128,6656]{1,0:T(8,128)(2,1)}), bf16[512,6656]{1,0:T(8,128)(2,1)}) %all-gather.7.cloned.1.call-update) | async-done | bytes 6815760 | tf_op jit(solution)/shard_map/all_gather | solution.py:65
  536.0 35.6 %fusion.10 = f32[512,4096]{1,0:T(8,128)} fusion(bf16[512,6656]{1,0:T(8,128)(2,1)} %all-gather.7.cloned.1.call-done, bf16[4096,6656]{1,0:T(8,128)(2,1)} %bitcast.20), kind=kOutput, calls=%fused_computation.29 | convolution fusion | flops 27917287424 | bytes 69730304 | tf_op jit(solution)/shard_map/dot_general | solution.py:69
  571.5 0.0 reduce-scatter.5.cloned.1.call-update
  571.5 0.0 all-gather.11.cloned.1.call-start
  571.6 0.5 all-gather.11.cloned.1.call-update
  572.1 0.0 all-gather.9.cloned.1.call-start
  572.2 0.1 dynamic_slice.9
  572.3 0.1 dynamic_slice.11
  572.3 69.1 %reduce-scatter.5.cloned.1.call-done = f32[64,4096]{1,0:T(8,128)} async-done(((f32[512,4096]{1,0:T(8,128)}), f32[64,4096]{1,0:T(8,128)}) %reduce-scatter.5.cloned.1.call-update) | async-done | bytes 1048592 | tf_op jit(solution)/shard_map/reduce_scatter | solution.py:68
  641.4 0.0 copy-start
  641.4 1.5 multiply_reduce_fusion.1
  642.9 11.7 %psum.23 = f32[64]{0:T(128)S(1)} all-reduce(f32[64]{0:T(128)S(1)} %multiply_reduce_fusion.1), channel_id=1, replica_groups=mesh['batch'=4,'hidden'=2,'width'=4] {'width'}, use_global_device_ids=true, to_apply=%region_6.7 | all-reduce | flops 64 | bytes 512 | tf_op jit(solution)/shard_map/psum | solution.py:81
  654.6 0.0 copy-done
  654.6 1.0 select_convert_fusion
  655.7 0.0 all-gather.9.cloned.1.call-update
  655.7 12.7 %all-gather.11.cloned.1.call-done = bf16[4,512,640]{2,1,0:T(8,128)(2,1)} async-done(((bf16[1,512,640]{2,1,0:T(8,128)(2,1)}), bf16[4,512,640]{2,1,0:T(8,128)(2,1)}) %all-gather.11.cloned.1.call-update) | async-done | bytes 2621456 | tf_op jit(solution)/shard_map/all_gather | solution.py:86
  668.4 5.3 reshape.70
  673.7 33.7 %all-gather.9.cloned.1.call-done = bf16[512,4096]{1,0:T(8,128)(2,1)} async-done(((bf16[64,4096]{1,0:T(8,128)(2,1)}), bf16[512,4096]{1,0:T(8,128)(2,1)}) %all-gather.9.cloned.1.call-update) | async-done | bytes 4194320 | tf_op jit(solution)/shard_map/all_gather | solution.py:91
  707.4 22.7 %fusion.11 = f32[4096,2560]{0,1:T(8,128)} fusion(bf16[512,4096]{1,0:T(8,128)(2,1)} %all-gather.9.cloned.1.call-done, bf16[512,2560]{1,0:T(8,128)(2,1)} %reshape.70), kind=kOutput, calls=%fused_computation.30 | convolution fusion | flops 10737418240 | bytes 48758784 | tf_op jit(solution)/shard_map/dot_general | solution.py:89
  (4 shorter events, 0.0 us)
Async XLA Ops:
  7.2 78.6 %all-reduce.2.cloned.1.call-start = ((), (), s32[]{:S(2)}) async-start(), calls=%async_computation.2 | async-start | bytes 4194304 | tf_op jit(solution)/shard_map/psum | solution.py:25
  19.9 1.5 copy-start.3
  19.9 65.9 %copy-start.1 = (bf16[128,4096]{1,0:T(8,128)(2,1)S(1)}, bf16[128,4096]{1,0:T(8,128)(2,1)}, u32[]{:S(2)}) copy-start(bf16[128,4096]{1,0:T(8,128)(2,1)} %param.10) | copy-start | bytes 3145732
  19.9 120.3 %all-gather.5.cloned.1.call-start = ((), (), s32[]{:S(2)}) async-start(), calls=%async_computation.3 | async-start | bytes 5242880 | tf_op jit(solution)/shard_map/all_gather | solution.py:46
  102.8 302.9 %reduce-scatter.3.cloned.1.call-start = ((), (), s32[]{:S(2)}) async-start(), calls=%async_computation.4 | async-start | bytes 17039360 | tf_op jit(solution)/shard_map/reduce_scatter | solution.py:50
  179.1 226.6 %copy-start.2 = (bf16[128,3328]{1,0:T(8,128)(2,1)S(1)}, bf16[128,3328]{1,0:T(8,128)(2,1)}, u32[]{:S(2)}) copy-start(bf16[128,3328]{1,0:T(8,128)(2,1)} %param.15) | copy-start | bytes 2555908
  179.1 356.8 %all-gather.7.cloned.1.call-start = ((), (), s32[]{:S(2)}) async-start(), calls=%async_computation.5 | async-start | bytes 8519680 | tf_op jit(solution)/shard_map/all_gather | solution.py:65
  410.9 230.5 %reduce-scatter.5.cloned.1.call-start = ((), (), s32[]{:S(2)}) async-start(), calls=%async_computation.6 | async-start | bytes 9437184 | tf_op jit(solution)/shard_map/reduce_scatter | solution.py:68
  571.5 96.8 %all-gather.11.cloned.1.call-start = ((), (), s32[]{:S(2)}) async-start(), calls=%async_computation.8 | async-start | bytes 3276800 | tf_op jit(solution)/shard_map/all_gather | solution.py:86
  572.1 135.3 %all-gather.9.cloned.1.call-start = ((), (), s32[]{:S(2)}) async-start(), calls=%async_computation.7 | async-start | bytes 4718592 | tf_op jit(solution)/shard_map/all_gather | solution.py:91
  641.4 13.2 %copy-start = (f32[64,4096]{1,0:T(8,128)S(1)}, f32[64,4096]{1,0:T(8,128)}, u32[]{:S(2)}) copy-start(f32[64,4096]{1,0:T(8,128)} %reduce-scatter.5.cloned.1.call-done) | copy-start | bytes 3145732
Sparse Core Ops, SparseCore 0:
  20.0 65.6 all-reduce.1
  102.9 31.6 all-gather.4
  179.3 226.3 reduce-scatter.2
  411.0 124.9 all-gather.6
  571.7 69.6 reduce-scatter.4
  642.8 25.5 all-gather.10
  670.8 36.5 all-gather.8
where the time goes:
time: 737 us
  waiting for transfers between devices  532 us (72%)
  matrix products  108 us (15%)
  local copies, waits for them, and re-layouts  44.4 us (6%)
  blocking collectives  23.4 us (3%)
  between operations  15.5 us (2%)
  other arithmetic  13 us (2%)
    reduce_scatter x1, waiting for transfers between devices, on_device(): lax.psum_scatter(partial_pair, 'width', scatter_dimension=0, tiled=True)  226 us
    all_gather x1, waiting for transfers between devices, on_device(): all_pairs = lax.all_gather(grad_pair, 'width', axis=0, tiled=True)  125 us
    reduce_scatter x1, waiting for transfers between devices, on_device(): lax.psum_scatter(lax.dot_general(row_block, weights, (((1,), (1,)), ((),...  69.1 us
    psum x1, waiting for transfers between devices, on_device(): audio_part = lax.psum(partial_audio, 'hidden')  64.4 us
    dot_general x1, matrix products, on_device(): jnp.dot(lax.all_gather(normed, 'batch', axis=0, tiled=True), weights, pre...  38.9 us
    unnamed x9, local copies, waits for them, and re-layouts  37.4 us
    dot_general x1, matrix products, on_device(): lax.dot_general(row_block, weights, (((1,), (1,)), ((), ())), preferred_e...  35.6 us
    all_gather x1, waiting for transfers between devices, on_device(): lax.all_gather(audio_grad, ('batch', 'hidden'), axis=0, tiled=True)  33.7 us
  transfers between devices with their start and end apart: 7, of which 6 were waited for; matrix products, arithmetic and copies ran while one was open for 6% of the time, Pallas kernels for 0%

commit v1 on v0

--- a/solution.py
+++ b/solution.py
@@ -22,7 +22,11 @@
     stacked = frames.reshape(tok_here, 4 * feat_here)
     kernel = adapter_weight.reshape(4 * feat_here, width_here)
     partial_audio = jnp.dot(stacked, kernel, preferred_element_type=jnp.float32)
-    audio_part = lax.psum(partial_audio, "hidden")
+
+    def name_ticks(xx, mesh_ax="hidden"):
+        return lax.all_gather(xx, mesh_ax).sum(axis=0)
+
+    audio_part = name_ticks(partial_audio)
     local_index = jnp.arange(tok_here, dtype=jnp.int32)
     row_index = local_index // seq_len
     positions = local_index % seq_len

time: 737 us -> 728 us (0.988)
    psum x1 -> x0, waiting for transfers between devices: 64.4 us -> none  [on_device(): audio_part = lax.psum(partial_audio, 'hidden')]
    all_gather x0 -> x1, waiting for transfers between devices: none -> 58.2 us  [name_ticks(): return lax.all_gather(xx, mesh_ax).sum(axis=0)]
    unnamed x9 -> x11, local copies, waits for them, and re-layouts: 37.4 us -> 37.7 us
where the time goes in v1:
time: 728 us
  waiting for transfers between devices  526 us (72%)
  matrix products  105 us (14%)
  local copies, waits for them, and re-layouts  43.5 us (6%)
  blocking collectives  23.6 us (3%)
  between operations  15.5 us (2%)
  other arithmetic  13.3 us (2%)
    reduce_scatter x1, waiting for transfers between devices, on_device(): lax.psum_scatter(partial_pair, 'width', scatter_dimension=0, tiled=True)  226 us
    all_gather x1, waiting for transfers between devices, on_device(): all_pairs = lax.all_gather(grad_pair, 'width', axis=0, tiled=True)  125 us
    reduce_scatter x1, waiting for transfers between devices, on_device(): lax.psum_scatter(lax.dot_general(row_block, weights, (((1,), (1,)), ((),...  69 us
    all_gather x1, waiting for transfers between devices, name_ticks(): return lax.all_gather(xx, mesh_ax).sum(axis=0)  58.2 us
    dot_general x1, matrix products, on_device(): jnp.dot(lax.all_gather(normed, 'batch', axis=0, tiled=True), weights, pre...  38.8 us
    unnamed x11, local copies, waits for them, and re-layouts  37.7 us
    dot_general x1, matrix products, on_device(): lax.dot_general(row_block, weights, (((1,), (1,)), ((), ())), preferred_e...  35.6 us
    all_gather x1, waiting for transfers between devices, on_device(): lax.all_gather(audio_grad, ('batch', 'hidden'), axis=0, tiled=True)  35 us
  transfers between devices with their start and end apart: 7, of which 6 were waited for; matrix products, arithmetic and copies ran while one was open for 6% of the time, Pallas kernels for 0%

profile of v1, /device:TPU:0, one launch (start us, length us, event | category | flops | bytes accessed | tf_op | source)
XLA Modules:
  0.0 728.0 jit_solution(12098308574365659535)
XLA Ops:
  7.2 0.0 all-gather.15.cloned.1.call-start
  7.2 1.5 reshape.67
  8.7 11.2 %fusion.8 = f32[128,4096]{1,0:T(8,128)} fusion(bf16[128,2560]{1,0:T(8,128)(2,1)S(1)} %reshape.67, bf16[2560,4096]{1,0:T(8,128)(2,1)} %bitcast.22), kind=kOutput, calls=%fused_computation.27 | convolution fusion | flops 2684354560 | bytes 23724032 | tf_op jit(solution)/shard_map/dot_general | solution.py:24
  19.9 0.0 copy-start.4
  19.9 0.0 all-gather.15.cloned.1.call-update
  19.9 0.0 all-gather.7.cloned.1.call-start
  21.3 0.0 copy-done.4
  21.3 58.2 %all-gather.15.cloned.1.call-done = f32[256,4096]{1,0:T(8,128)} async-done(((f32[128,4096]{1,0:T(8,128)}), f32[256,4096]{1,0:T(8,128)}) %all-gather.15.cloned.1.call-update) | async-done | bytes 4194320 | tf_op jit(solution)/shard_map/all_gather | solution.py:27
  79.5 0.0 copy-start.2
  79.5 2.8 reduce_sum.27
  82.3 0.0 copy-done.2
  82.3 0.5 multiply_reduce_fusion
  82.8 11.7 %psum.14 = f32[128]{0:T(128)S(1)} all-reduce(f32[128]{0:T(128)S(1)} %multiply_reduce_fusion), channel_id=1, replica_groups=mesh['batch'=4,'hidden'=2,'width'=4] {'width'}, use_global_device_ids=true, to_apply=%region_2.3 | all-reduce | flops 128 | bytes 1024 | tf_op jit(solution)/shard_map/psum | solution.py:42
  94.5 2.3 multiply_convert_fusion
  96.8 0.0 all-gather.7.cloned.1.call-update
  96.8 0.2 reduce-scatter.3.cloned.1.call-start
  97.0 37.7 %copy.10 = bf16[512,8,2,3328]{3,1,2,0:T(8,128)(2,1)} copy(bf16[512,8,2,3328]{3,2,1,0:T(2,128)(2,1)} %bitcast.19) | data formatting | bytes 109051904
  134.7 0.0 all-gather.7.cloned.1.call-done
  134.7 38.8 %fusion.9 = f32[512,6656]{1,0:T(8,128)} fusion(bf16[512,4096]{1,0:T(8,128)(2,1)} %all-gather.7.cloned.1.call-done, bf16[4096,6656]{1,0:T(8,128)(2,1)} %bitcast.20), kind=kOutput, calls=%fused_computation.28 | convolution fusion | flops 27917287424 | bytes 72351744 | tf_op jit(solution)/shard_map/dot_general | solution.py:49
  173.5 0.0 copy-start.3
  173.5 0.0 reduce-scatter.3.cloned.1.call-update
  173.5 0.0 all-gather.9.cloned.1.call-start
  173.6 226.0 %reduce-scatter.3.cloned.1.call-done = f32[128,6656]{1,0:T(8,128)} async-done(((f32[512,6656]{1,0:T(8,128)}), f32[128,6656]{1,0:T(8,128)}) %reduce-scatter.3.cloned.1.call-update) | async-done | bytes 3407888 | tf_op jit(solution)/shard_map/reduce_scatter | solution.py:54
  399.6 0.0 copy-done.3
  399.6 3.9 fusion.1
  403.5 1.3 pad_maximum_fusion
  404.8 0.0 all-gather.9.cloned.1.call-update
  404.8 0.0 reduce-scatter.5.cloned.1.call-start
  404.8 125.1 %all-gather.9.cloned.1.call-done = bf16[512,6656]{1,0:T(8,128)(2,1)} async-done(((bf16[128,6656]{1,0:T(8,128)(2,1)}), bf16[512,6656]{1,0:T(8,128)(2,1)}) %all-gather.9.cloned.1.call-update) | async-done | bytes 6815760 | tf_op jit(solution)/shard_map/all_gather | solution.py:69
  529.9 35.6 %fusion.10 = f32[512,4096]{1,0:T(8,128)} fusion(bf16[512,6656]{1,0:T(8,128)(2,1)} %all-gather.9.cloned.1.call-done, bf16[4096,6656]{1,0:T(8,128)(2,1)} %bitcast.21), kind=kOutput, calls=%fused_computation.29 | convolution fusion | flops 27917287424 | bytes 69730304 | tf_op jit(solution)/shard_map/dot_general | solution.py:73
  565.5 0.0 copy-start
  565.5 0.0 reduce-scatter.5.cloned.1.call-update
  565.5 0.0 all-gather.13.cloned.1.call-start
  565.6 0.5 all-gather.13.cloned.1.call-update
  566.1 0.0 all-gather.11.cloned.1.call-start
  566.1 0.1 dynamic_slice.9
  566.2 0.1 dynamic_slice.11
  566.3 69.0 %reduce-scatter.5.cloned.1.call-done = f32[64,4096]{1,0:T(8,128)} async-done(((f32[512,4096]{1,0:T(8,128)}), f32[64,4096]{1,0:T(8,128)}) %reduce-scatter.5.cloned.1.call-update) | async-done | bytes 1048592 | tf_op jit(solution)/shard_map/reduce_scatter | solution.py:72
  635.3 0.0 copy-start.1
  635.3 0.0 copy-done
  635.3 1.5 multiply_reduce_fusion.1
  636.9 11.9 %psum.15 = f32[64]{0:T(128)S(1)} all-reduce(f32[64]{0:T(128)S(1)} %multiply_reduce_fusion.1), channel_id=1, replica_groups=mesh['batch'=4,'hidden'=2,'width'=4] {'width'}, use_global_device_ids=true, to_apply=%region_6.7 | all-reduce | flops 64 | bytes 512 | tf_op jit(solution)/shard_map/psum | solution.py:85
  648.8 0.0 copy-done.1
  648.8 1.0 select_convert_fusion
  649.8 0.0 all-gather.11.cloned.1.call-update
  649.9 12.5 %all-gather.13.cloned.1.call-done = bf16[4,512,640]{2,1,0:T(8,128)(2,1)} async-done(((bf16[1,512,640]{2,1,0:T(8,128)(2,1)}), bf16[4,512,640]{2,1,0:T(8,128)(2,1)}) %all-gather.13.cloned.1.call-update) | async-done | bytes 2621456 | tf_op jit(solution)/shard_map/all_gather | solution.py:90
  662.3 4.1 reshape.70
  666.4 35.0 %all-gather.11.cloned.1.call-done = bf16[512,4096]{1,0:T(8,128)(2,1)} async-done(((bf16[64,4096]{1,0:T(8,128)(2,1)}), bf16[512,4096]{1,0:T(8,128)(2,1)}) %all-gather.11.cloned.1.call-update) | async-done | bytes 4194320 | tf_op jit(solution)/shard_map/all_gather | solution.py:95
  701.4 19.7 %fusion.11 = f32[4096,2560]{0,1:T(8,128)} fusion(bf16[512,4096]{1,0:T(8,128)(2,1)} %all-gather.11.cloned.1.call-done, bf16[512,2560]{1,0:T(8,128)(2,1)S(1)} %reshape.70), kind=kOutput, calls=%fused_computation.30 | convolution fusion | flops 10737418240 | bytes 48758784 | tf_op jit(solution)/shard_map/dot_general | solution.py:93
  (4 shorter events, 0.0 us)
Async XLA Ops:
  7.2 72.4 %all-gather.15.cloned.1.call-start = ((), (), s32[]{:S(2)}) async-start(), calls=%async_computation.8 | async-start | bytes 6291456 | tf_op jit(solution)/shard_map/all_gather | solution.py:27
  19.9 1.4 copy-start.4
  19.9 114.8 %all-gather.7.cloned.1.call-start = ((), (), s32[]{:S(2)}) async-start(), calls=%async_computation.2 | async-start | bytes 5242880 | tf_op jit(solution)/shard_map/all_gather | solution.py:50
  79.5 2.8 copy-start.2
  96.8 302.8 %reduce-scatter.3.cloned.1.call-start = ((), (), s32[]{:S(2)}) async-start(), calls=%async_computation.3 | async-start | bytes 17039360 | tf_op jit(solution)/shard_map/reduce_scatter | solution.py:54
  173.5 226.1 %copy-start.3 = (bf16[128,3328]{1,0:T(8,128)(2,1)S(1)}, bf16[128,3328]{1,0:T(8,128)(2,1)}, u32[]{:S(2)}) copy-start(bf16[128,3328]{1,0:T(8,128)(2,1)} %param.15) | copy-start | bytes 2555908
  173.5 356.4 %all-gather.9.cloned.1.call-start = ((), (), s32[]{:S(2)}) async-start(), calls=%async_computation.4 | async-start | bytes 8519680 | tf_op jit(solution)/shard_map/all_gather | solution.py:69
  404.8 230.5 %reduce-scatter.5.cloned.1.call-start = ((), (), s32[]{:S(2)}) async-start(), calls=%async_computation.5 | async-start | bytes 9437184 | tf_op jit(solution)/shard_map/reduce_scatter | solution.py:72
  565.5 69.9 %copy-start = (f32[128,4096]{1,0:T(8,128)S(1)}, f32[128,4096]{1,0:T(8,128)}, u32[]{:S(2)}) copy-start(f32[128,4096]{1,0:T(8,128)} %get-tuple-element.3) | copy-start | bytes 6291460
  565.5 96.8 %all-gather.13.cloned.1.call-start = ((), (), s32[]{:S(2)}) async-start(), calls=%async_computation.7 | async-start | bytes 3276800 | tf_op jit(solution)/shard_map/all_gather | solution.py:90
  566.1 135.3 %all-gather.11.cloned.1.call-start = ((), (), s32[]{:S(2)}) async-start(), calls=%async_computation.6 | async-start | bytes 4718592 | tf_op jit(solution)/shard_map/all_gather | solution.py:95
  635.3 13.5 %copy-start.1 = (f32[64,4096]{1,0:T(8,128)S(1)}, f32[64,4096]{1,0:T(8,128)}, u32[]{:S(2)}) copy-start(f32[64,4096]{1,0:T(8,128)} %reduce-scatter.5.cloned.1.call-done) | copy-start | bytes 3145732
Sparse Core Ops, SparseCore 0:
  20.0 59.4 all-gather.14
  96.9 31.6 all-gather.6
  173.7 225.9 reduce-scatter.2
  404.9 124.9 all-gather.8
  565.6 69.6 reduce-scatter.4
  636.7 25.5 all-gather.12
  664.8 36.5 all-gather.10
